TPU v7x, 32 devices: a whole 2x2x4 slice. The times are simulated.
32 devices in a mesh: dp: 4 (over y, core), vocab: 8 (over z, x).
Axes of the slice: x: 2, y: 2, z: 4, core: 2. Of those that a mesh axis runs over, the one named last changes fastest.
Arguments:
- student_hidden: bfloat16 [2048, 2048], P('dp', 'vocab'), may hold values from -150 to 150
- teacher_hidden: bfloat16 [2048, 2048], P('dp', 'vocab'), may hold values from -150 to 150
- head: bfloat16 [2048, 16384], P(None, 'vocab'), may hold values from -0.375 to 0.375
- mask: int32 [2048], P('dp'), may hold values from 0 to 1
- steps: int32 [16], P('dp'), may hold values from 1 to 8
Outputs:
- divergence: float32 [2048], P('dp')
- hidden_grad: bfloat16 [2048, 2048], P('dp', 'vocab')
All inputs are finite; a program needn't handle non-finite values.
Results may differ from a plain program's by a relative error of at most 0.0051.
Values may be sent and summed in bfloat16 or wider, within the bound.
A program may use at most 64 MiB of HBM per device.

v0:
```python
import jax
import jax.numpy as jnp
from jax import lax
from jax.sharding import PartitionSpec as P

LENGTH = 128
STEPS = 8


def fold_stats(spread):
    student_peak = jnp.max(spread[0], axis=0)
    teacher_peak = jnp.max(spread[2], axis=0)
    student_scale = jnp.exp(spread[0] - student_peak[None, :])
    teacher_scale = jnp.exp(spread[2] - teacher_peak[None, :])
    return (
        student_peak,
        jnp.sum(spread[1] * student_scale, axis=0),
        teacher_peak,
        jnp.sum(spread[3] * teacher_scale, axis=0),
        jnp.sum(spread[4] * teacher_scale, axis=0),
    )


def per_device(student_hidden, teacher_hidden, head, mask, steps):
    rows = mask.shape[0]
    masked = mask.astype(jnp.float32)
    count = lax.psum(jnp.sum(masked), "dp")
    factor = jnp.repeat(STEPS / steps.astype(jnp.float32), LENGTH)
    weight = masked * factor * (rows * lax.axis_size("dp") / jnp.maximum(count, 1.0))
    student_full, teacher_full = (
        lax.all_gather(student_hidden, "vocab", axis=1, tiled=True),
        lax.all_gather(teacher_hidden, "vocab", axis=1, tiled=True),
    )
    student_log = jnp.dot(student_full, head, preferred_element_type=jnp.float32)
    teacher_log = jnp.dot(teacher_full, head, preferred_element_type=jnp.float32)
    student_local = jnp.max(student_log, axis=1)
    teacher_local = jnp.max(teacher_log, axis=1)
    student_exp = jnp.exp(student_log - student_local[:, None])
    teacher_exp = jnp.exp(teacher_log - teacher_local[:, None])
    student_sum = jnp.sum(student_exp, axis=1)
    teacher_sum = jnp.sum(teacher_exp, axis=1)
    cross_sum = jnp.sum(teacher_exp * (teacher_log - student_log), axis=1)
    spread = (
        lax.all_gather(student_local[None, :], "vocab", axis=0, tiled=True),
        lax.all_gather(student_sum[None, :], "vocab", axis=0, tiled=True),
        lax.all_gather(teacher_local[None, :], "vocab", axis=0, tiled=True),
        lax.all_gather(teacher_sum[None, :], "vocab", axis=0, tiled=True),
        lax.all_gather(cross_sum[None, :], "vocab", axis=0, tiled=True),
    )
    merged = fold_stats(spread)
    student_peak, student_total, teacher_peak, teacher_total, cross = merged
    divergence = (
        cross / teacher_total
        - (teacher_peak + jnp.log(teacher_total))
        + (student_peak + jnp.log(student_total))
    )
    student_prob = student_exp * (jnp.exp(student_local - student_peak) / student_total)[:, None]
    teacher_prob = teacher_exp * (jnp.exp(teacher_local - teacher_peak) / teacher_total)[:, None]
    slopes = (weight[:, None] * (student_prob - teacher_prob)).astype(jnp.bfloat16)
    summed = lax.psum_scatter(
        lax.dot_general(head, slopes, (((1,), (1,)), ((), ())), preferred_element_type=jnp.float32),
        "vocab",
        scatter_dimension=0,
        tiled=True,
    )
    hidden_grad = summed.T.astype(jnp.bfloat16)
    return (divergence, hidden_grad)


def solution(mesh):
    placed = (P("dp", "vocab"), P("dp", "vocab"), P(None, "vocab"), P("dp"), P("dp"))
    return jax.shard_map(
        per_device,
        mesh=mesh,
        in_specs=placed,
        out_specs=(P("dp"), P("dp", "vocab")),
        check_vma=False,
    )
```

profile of v0, /device:TPU:0, one launch (start us, length us, event | category | flops | bytes accessed | tf_op | source)
XLA Modules:
  0.0 336.2 jit_solution(18111818098604635555)
XLA Ops:
  7.2 0.0 all-gather.13.cloned.1.call-start
  7.2 0.7 all-gather.13.cloned.1.call-update
  7.9 0.0 all-gather.15.cloned.1.call-start
  7.9 0.7 all-gather.15.cloned.1.call-update
  8.6 0.0 reduce-scatter.2.cloned.1.call-start
  8.7 1.3 convert_reduce_fusion
  10.0 9.0 %psum.7 = f32[]{:T(128)} all-reduce(f32[]{:T(128)} %convert_reduce_fusion), channel_id=1, replica_groups=mesh['dp'=4,'vocab'=8] {'dp'}, use_global_device_ids=true, to_apply=%region_11.0 | all-reduce | flops 1 | bytes 8 | tf_op jit(solution)/shard_map/psum | solution.py:27
  19.7 0.7 convert_divide_fusion
  20.3 0.8 fusion.13
  21.1 42.0 %all-gather.13.cloned.1.call-done = bf16[512,2048]{1,0:T(8,128)(2,1)} async-done(((bf16[512,256]{1,0:T(8,128)(2,1)}), bf16[512,2048]{1,0:T(8,128)(2,1)}) %all-gather.13.cloned.1.call-update) | async-done | bytes 2097168 | tf_op jit(solution)/shard_map/all_gather | solution.py:32
  63.1 10.4 %fusion.15 = (f32[512]{0:T(512)S(1)}, f32[512,2048]{1,0:T(8,128)}) fusion(bf16[512,2048]{1,0:T(8,128)(2,1)} %all-gather.13.cloned.1.call-done, bf16[2048,2048]{1,0:T(8,128)(2,1)} %param.7), kind=kOutput, calls=%fused_computation.31 | convolution fusion | flops 4296015360 | bytes 14682112 | tf_op jit(solution)/shard_map/dot_general | solution.py:35
  73.6 26.6 %all-gather.6 = f32[8,1,512]{2,1,0:T(1,128)S(1)} all-gather(f32[1,1,512]{2,1,0:T(1,128)S(1)} %bitcast.44), channel_id=3, replica_groups=mesh['dp'=4,'vocab'=8] {'vocab'}, dimensions={0}, use_global_device_ids=true | all-gather | bytes 18432 | tf_op jit(solution)/shard_map/all_gather | solution.py:46
  100.1 13.7 %all-gather.15.cloned.1.call-done = bf16[512,2048]{1,0:T(8,128)(2,1)} async-done(((bf16[512,256]{1,0:T(8,128)(2,1)}), bf16[512,2048]{1,0:T(8,128)(2,1)}) %all-gather.15.cloned.1.call-update) | async-done | bytes 2097168 | tf_op jit(solution)/shard_map/all_gather | solution.py:31
  113.8 7.8 %fusion.14 = (f32[512]{0:T(512)S(1)}, f32[512,2048]{1,0:T(8,128)S(1)}) fusion(bf16[512,2048]{1,0:T(8,128)(2,1)} %all-gather.15.cloned.1.call-done, bf16[2048,2048]{1,0:T(8,128)(2,1)} %param.7), kind=kOutput, calls=%fused_computation.30 | convolution fusion | flops 4296015360 | bytes 14682112 | tf_op jit(solution)/shard_map/dot_general | solution.py:34
  121.7 2.1 multiply_reduce_fusion
  123.8 26.1 %all-gather.7 = f32[8,1,512]{2,1,0:T(1,128)S(1)} all-gather(f32[1,1,512]{2,1,0:T(1,128)S(1)} %bitcast.48), channel_id=4, replica_groups=mesh['dp'=4,'vocab'=8] {'vocab'}, dimensions={0}, use_global_device_ids=true | all-gather | bytes 18432 | tf_op jit(solution)/shard_map/all_gather | solution.py:47
  149.9 26.1 %all-gather.5 = f32[8,1,512]{2,1,0:T(1,128)S(1)} all-gather(f32[1,1,512]{2,1,0:T(1,128)S(1)} %bitcast.47), channel_id=2, replica_groups=mesh['dp'=4,'vocab'=8] {'vocab'}, dimensions={0}, use_global_device_ids=true | all-gather | bytes 18432 | tf_op jit(solution)/shard_map/all_gather | solution.py:48
  176.0 26.1 %all-gather.8 = f32[8,1,512]{2,1,0:T(1,128)S(1)} all-gather(f32[1,1,512]{2,1,0:T(1,128)S(1)} %bitcast.45), channel_id=5, replica_groups=mesh['dp'=4,'vocab'=8] {'vocab'}, dimensions={0}, use_global_device_ids=true | all-gather | bytes 18432 | tf_op jit(solution)/shard_map/all_gather | solution.py:44
  202.2 26.1 %all-gather.9 = f32[8,1,512]{2,1,0:T(1,128)S(1)} all-gather(f32[1,1,512]{2,1,0:T(1,128)S(1)} %bitcast.46), channel_id=6, replica_groups=mesh['dp'=4,'vocab'=8] {'vocab'}, dimensions={0}, use_global_device_ids=true | all-gather | bytes 18432 | tf_op jit(solution)/shard_map/all_gather | solution.py:45
  228.4 0.6 exponential_divide_fusion.1
  229.0 12.8 %convolution_bitcast_fusion = f32[2048,512]{0,1:T(8,128)} fusion(bf16[2048,2048]{1,0:T(8,128)(2,1)} %param.7, f32[512,2048]{1,0:T(8,128)} %get-tuple-element.13, f32[512,2048]{1,0:T(8,128)} %copy-done.1, f32[512]{0:T(512)S(1)} %get-tuple-element.9, f32[512]{0:T(512)S(1)} %get-tuple-element.7, f32[512]{0:T(512)S(1)} %fusion.13, ...), kind=kOutput, calls=%fused_computation.6 | convolution fusion | flops 4302307328 | bytes 20981760 | tf_op jit(solution)/shard_map/dot_general | solution.py:61
  241.8 0.0 reduce-scatter.2.cloned.1.call-update
  241.8 86.1 %reduce-scatter.2.cloned.1.call-done = f32[256,512]{0,1:T(8,128)} async-done(((f32[2048,512]{0,1:T(8,128)}), f32[256,512]{0,1:T(8,128)}) %reduce-scatter.2.cloned.1.call-update) | async-done | bytes 524304 | tf_op jit(solution)/shard_map/reduce_scatter | solution.py:60
  327.9 1.8 convert_bitcast_fusion
  (8 shorter events, 0.1 us)
Async XLA Ops:
  7.2 56.0 %all-gather.13.cloned.1.call-start = ((), (), s32[]{:S(2)}) async-start(), calls=%async_computation.1 | async-start | bytes 2359296 | tf_op jit(solution)/shard_map/all_gather | solution.py:32
  7.9 105.9 %all-gather.15.cloned.1.call-start = ((), (), s32[]{:S(2)}) async-start(), calls=%async_computation.2 | async-start | bytes 2359296 | tf_op jit(solution)/shard_map/all_gather | solution.py:31
  8.6 319.2 %reduce-scatter.2.cloned.1.call-start = ((), (), s32[]{:S(2)}) async-start(), calls=%async_computation.3 | async-start | bytes 4718592 | tf_op jit(solution)/shard_map/reduce_scatter | solution.py:60
  113.8 7.9 %copy-start = (f32[512,2048]{1,0:T(8,128)S(1)}, f32[512,2048]{1,0:T(8,128)}, u32[]{:S(2)}) copy-start(f32[512,2048]{1,0:T(8,128)} %get-tuple-element.13) | copy-start | bytes 12582916
  121.7 2.1 copy-start.1
Sparse Core Ops, SparseCore 0:
  10.0 53.0 all-gather.12
  65.2 48.6 all-gather.14
  241.9 85.9 reduce-scatter.1
where the time goes:
time: 336 us
  waiting for transfers between devices  143 us (43%)
  blocking collectives  140 us (42%)
  matrix products  31.1 us (9%)
  between operations  14.5 us (4%)
  other arithmetic  7.27 us (2%)
    reduce_scatter x1, waiting for transfers between devices, per_device(): lax.psum_scatter(lax.dot_general(head, slopes, (((1,), (1,)), ((), ())),...  86.1 us
    all_gather x1, waiting for transfers between devices, per_device(): lax.all_gather(teacher_hidden, 'vocab', axis=1, tiled=True)  42 us
    all_gather x1, blocking collectives, per_device(): lax.all_gather(teacher_local[None, :], 'vocab', axis=0, tiled=True)  26.6 us
    all_gather x1, blocking collectives, per_device(): lax.all_gather(student_sum[None, :], 'vocab', axis=0, tiled=True)  26.1 us
    all_gather x1, blocking collectives, per_device(): lax.all_gather(teacher_sum[None, :], 'vocab', axis=0, tiled=True)  26.1 us
    all_gather x1, blocking collectives, per_device(): lax.all_gather(student_local[None, :], 'vocab', axis=0, tiled=True)  26.1 us
    all_gather x1, blocking collectives, per_device(): lax.all_gather(cross_sum[None, :], 'vocab', axis=0, tiled=True)  26.1 us
    all_gather x1, waiting for transfers between devices, per_device(): lax.all_gather(student_hidden, 'vocab', axis=1, tiled=True)  13.7 us
  transfers between devices with their start and end apart: 3, of which 3 were waited for; matrix products, arithmetic and copies ran while one was open for 4% of the time, Pallas kernels for 0%

commit v1 on v0

v1 whole, which is shorter than its diff:
```python
import functools

import jax
import jax.numpy as jnp
from jax import lax
from jax.experimental import pallas as pl
from jax.experimental.pallas import tpu as pltpu
from jax.sharding import PartitionSpec as P

MESH = pl.DeviceIdType.MESH
STEPS = 8
F32, BF16 = jnp.float32, jnp.bfloat16


def loop(start, stop, body):
    lax.fori_loop(start, stop, lambda i, carry: (body(i), carry)[1], 0)


def kernel(
    n, ndp, s_ref, t_ref, head_hbm, mask_ref, steps_ref, div_ref, grad_ref,
    head, s_all, t_all, s_log, t_log, slopes, cols, stats, counts, g, rs_out, rs_in,
    head_sem, ag_send, ag_recv, st_send, st_recv, ct_send, ct_recv, rs_send, rs_recv,
):
    T, F = s_ref.shape
    V = head.shape[1]
    H = n // 2
    C = T // 2
    me = lax.axis_index("vocab")
    dp = lax.axis_index("dp")

    def at_pos(q):
        q = lax.rem(q + 2 * n, n)
        x = q // H
        z = q + x * (n - 1 - 2 * q)
        return 2 * z + x

    z0, x0 = me // 2, lax.rem(me, 2)
    pos = z0 + x0 * (n - 1 - 2 * z0)
    ways = ((1, at_pos(pos + 1)), (-1, at_pos(pos - 1)))

    head_copy = pltpu.make_async_copy(head_hbm, head, head_sem)
    head_copy.start()

    count = jnp.sum(mask_ref[...].astype(F32), axis=1, keepdims=True)
    counts[dp] = jnp.broadcast_to(count, counts.shape[1:])

    barrier = pltpu.get_barrier_semaphore()
    for j in range(1, n):
        pl.semaphore_signal(barrier, 1, device_id={"vocab": lax.rem(me + j, n)}, device_id_type=MESH)
    for j in range(1, ndp):
        pl.semaphore_signal(barrier, 1, device_id={"dp": lax.rem(dp + j, ndp)}, device_id_type=MESH)
    pl.semaphore_wait(barrier, n - 1 + ndp - 1)

    def hop(way, h, which):
        step, target = ways[way]
        block = at_pos(pos - step * (h - 1))
        everything, own = ((s_all, s_ref), (t_all, t_ref))[which]
        source = own if isinstance(h, int) and h == 1 else everything.at[block]
        return pltpu.make_async_remote_copy(
            src_ref=source,
            dst_ref=everything.at[block],
            send_sem=ag_send.at[way, h, which],
            recv_sem=ag_recv.at[way, h, which],
            device_id={"vocab": target},
            device_id_type=MESH,
        )

    def arrived(way, h, which):
        hop(way, h, which).wait_recv()
        return at_pos(pos - ways[way][0] * h)

    for which in (0, 1):
        for way in (0, 1):
            hop(way, 1, which).start()

    def count_copy(j):
        return pltpu.make_async_remote_copy(
            src_ref=counts.at[dp],
            dst_ref=counts.at[dp],
            send_sem=ct_send.at[j],
            recv_sem=ct_recv.at[j],
            device_id={"dp": lax.rem(dp + j, ndp)},
            device_id_type=MESH,
        )

    for j in range(1, ndp):
        count_copy(j).start()

    W = 256

    def rows_of(block):
        return pl.ds(pl.multiple_of(block * F, F), F)

    def accumulate(log, parts, first=False):
        def tile(c):
            span = pl.ds(pl.multiple_of(c * W, W), W)
            total = None if first else log[:, span]
            for ref, block in parts:
                term = jnp.dot(ref[...], head[rows_of(block), span], preferred_element_type=F32)
                total = term if total is None else total + term
            log[:, span] = total

        loop(0, V // W, tile)

    head_copy.wait()
    accumulate(s_log, ((s_ref, me),), True)
    accumulate(t_log, ((t_ref, me),), True)

    def middle(h):
        for which, (everything, log) in enumerate(((s_all, s_log), (t_all, t_log))):
            found = []
            for way in (0, 1):
                block = arrived(way, h, which)
                if way == which:
                    hop(way, h + 1, which).start()
                else:
                    @pl.when(h + 1 < H)
                    def _():
                        hop(way, h + 1, which).start()
                found.append((everything.at[block], block))
            accumulate(log, found)

    loop(1, H, middle)
    block = arrived(0, H, 0)
    accumulate(s_log, ((s_all.at[block], block),))
    block = arrived(1, H, 1)
    accumulate(t_log, ((t_all.at[block], block),))

    R = 16
    lane = lax.broadcasted_iota(jnp.int32, (R, 128), 1)

    def softmax_rows(r):
        span = pl.ds(pl.multiple_of(r * R, R), R)
        s, t = s_log[span, :], t_log[span, :]
        s_peak = jnp.max(s, axis=1, keepdims=True)
        t_peak = jnp.max(t, axis=1, keepdims=True)
        s_exp = jnp.exp(s - s_peak)
        t_exp = jnp.exp(t - t_peak)
        cross = jnp.sum(t_exp * (t - s), axis=1, keepdims=True)
        s_log[span, :] = s_exp
        t_log[span, :] = t_exp
        s_sum = jnp.sum(s_exp, axis=1, keepdims=True)
        t_sum = jnp.sum(t_exp, axis=1, keepdims=True)
        value = jnp.where(lane == 0, s_peak, jnp.where(lane == 1, s_sum, jnp.where(
            lane == 2, t_peak, jnp.where(lane == 3, t_sum, cross))))
        cols[span, :] = value

    loop(0, T // R, softmax_rows)
    stats[me] = cols[...].T[:8, :]

    def stat_copy(j):
        return pltpu.make_async_remote_copy(
            src_ref=stats.at[me],
            dst_ref=stats.at[me],
            send_sem=st_send.at[j],
            recv_sem=st_recv.at[j],
            device_id={"vocab": lax.rem(me + j, n)},
            device_id_type=MESH,
        )

    for j in range(1, n):
        stat_copy(j).start()

    for j in range(1, ndp):
        count_copy(j).wait_recv()
    total = counts[0, :1, :1]
    for j in range(1, ndp):
        total = total + counts[j, :1, :1]
    segments = steps_ref.shape[0]
    factor = jnp.concatenate(
        [STEPS / jnp.full((1, T // segments), steps_ref[i], jnp.int32).astype(F32) for i in range(segments)], axis=1
    )
    weight = mask_ref[...].astype(F32) * factor * (T * ndp / jnp.maximum(total, 1.0))

    for j in range(1, n):
        stat_copy(j).wait_recv()
    s_top = stats[0, 0:1, :]
    t_top = stats[0, 2:3, :]
    for k in range(1, n):
        s_top = jnp.maximum(s_top, stats[k, 0:1, :])
        t_top = jnp.maximum(t_top, stats[k, 2:3, :])
    s_total = jnp.zeros((1, T), F32)
    t_total = jnp.zeros((1, T), F32)
    cross = jnp.zeros((1, T), F32)
    for k in range(n):
        t_scale = jnp.exp(stats[k, 2:3, :] - t_top)
        s_total += stats[k, 1:2, :] * jnp.exp(stats[k, 0:1, :] - s_top)
        t_total += stats[k, 3:4, :] * t_scale
        cross += stats[k, 4:5, :] * t_scale
    div_ref[...] = cross / t_total - (t_top + jnp.log(t_total)) + (s_top + jnp.log(s_total))
    mine = stats[me]
    s_factor = weight * (jnp.exp(mine[0:1, :] - s_top) / s_total)
    t_factor = weight * (jnp.exp(mine[2:3, :] - t_top) / t_total)
    row = lax.broadcasted_iota(jnp.int32, (128, T), 0)
    cols[...] = jnp.where(row == 0, s_factor, t_factor).T

    def slope_rows(r):
        span = pl.ds(pl.multiple_of(r * R, R), R)
        slopes[span, :] = (s_log[span, :] * cols[span, 0:1] - t_log[span, :] * cols[span, 1:2]).astype(BF16)

    loop(0, T // R, slope_rows)

    def part(block, c):
        return lax.dot_general(
            slopes[c * C:(c + 1) * C, :], head[rows_of(block), :], (((1,), (1,)), ((), ())), preferred_element_type=F32
        )

    def pass_on(way, k, c):
        return pltpu.make_async_remote_copy(
            src_ref=rs_out.at[way, k, c],
            dst_ref=rs_in.at[way, k, c],
            send_sem=rs_send.at[way, k, c],
            recv_sem=rs_recv.at[way, k, c],
            device_id={"vocab": ways[way][1]},
            device_id_type=MESH,
        )

    far = at_pos(pos + H)
    for c in (0, 1):
        rs_out[c, H, c] = part(far, c).astype(BF16)
        pass_on(c, H, c).start()

    def fill(k):
        for way in (0, 1):
            block = at_pos(pos + ways[way][0] * k)
            for c in (0, 1):
                g[way, c] = part(block, c)

    for way in (0, 1):
        block = at_pos(pos + ways[way][0] * (H - 1))
        c = 1 - way
        rs_out[way, H - 1, c] = part(block, c).astype(BF16)
        pass_on(way, H - 1, c).start()
        g[way, way] = part(block, way)
    for way in (0, 1):
        pass_on(way, H, way).wait_recv()
        rs_out[way, H - 1, way] = (g[way, way] + rs_in[way, H, way].astype(F32)).astype(BF16)
        pass_on(way, H - 1, way).start()

    def relay(i):
        k = H - 2 - i
        fill(k)
        for late in (0, 1):
            for way in (0, 1):
                c = 1 - way if late == 0 else way
                pass_on(way, k + 1, c).wait_recv()
                rs_out[way, k, c] = (g[way, c] + rs_in[way, k + 1, c].astype(F32)).astype(BF16)
                pass_on(way, k, c).start()

    loop(0, H - 2, relay)
    for c in (0, 1):
        g[0, c] = part(me, c)
    for c in (0, 1):
        for way in (0, 1):
            pass_on(way, 1, c).wait_recv()
        grad_ref[c * C:(c + 1) * C, :] = (
            g[0, c] + rs_in[0, 1, c].astype(F32) + rs_in[1, 1, c].astype(F32)
        ).astype(BF16)

    def left(h):
        for way in (0, 1):
            for which in (0, 1):
                hop(way, h, which).wait_send()

    for way in (0, 1):
        for which in (0, 1):
            hop(way, 1, which).wait_send()
    loop(2, H, left)
    for way in (0, 1):
        hop(way, H, way).wait_send()
    for j in range(1, ndp):
        count_copy(j).wait_send()
    for j in range(1, n):
        stat_copy(j).wait_send()
    for c in (0, 1):
        pass_on(c, H, c).wait_send()

    def gone(k):
        for way in (0, 1):
            for c in (0, 1):
                pass_on(way, k, c).wait_send()

    loop(1, H, gone)


def solution(mesh):
    n, ndp = mesh.shape["vocab"], mesh.shape["dp"]

    def per_device(student, teacher, head, mask, steps):
        T, F = student.shape
        D, V = head.shape
        H = n // 2
        vmem = pl.BlockSpec(memory_space=pltpu.VMEM)
        dma = pltpu.SemaphoreType.DMA
        div, grad = pl.pallas_call(
            functools.partial(kernel, n, ndp),
            out_shape=(jax.ShapeDtypeStruct((1, T), F32), jax.ShapeDtypeStruct((T, F), BF16)),
            in_specs=[vmem, vmem, pl.BlockSpec(memory_space=pl.ANY), vmem, pl.BlockSpec(memory_space=pltpu.SMEM)],
            out_specs=(vmem, vmem),
            scratch_shapes=[
                pltpu.VMEM((D, V), BF16),
                pltpu.VMEM((n, T, F), BF16),
                pltpu.VMEM((n, T, F), BF16),
                pltpu.VMEM((T, V), F32),
                pltpu.VMEM((T, V), F32),
                pltpu.VMEM((T, V), BF16),
                pltpu.VMEM((T, 128), F32),
                pltpu.VMEM((n, 8, T), F32),
                pltpu.VMEM((ndp, 8, 128), F32),
                pltpu.VMEM((2, 2, T // 2, F), F32),
                pltpu.VMEM((2, H + 1, 2, T // 2, F), BF16),
                pltpu.VMEM((2, H + 1, 2, T // 2, F), BF16),
                dma,
                dma((2, H + 1, 2)),
                dma((2, H + 1, 2)),
                dma((n,)),
                dma((n,)),
                dma((ndp,)),
                dma((ndp,)),
                dma((2, H + 1, 2)),
                dma((2, H + 1, 2)),
            ],
            compiler_params=pltpu.CompilerParams(
                collective_id=0, has_side_effects=True, vmem_limit_bytes=60 * 1024 * 1024
            ),
        )(student, teacher, head, mask.reshape(1, T), steps)
        return div.reshape(T), grad

    return jax.shard_map(
        per_device,
        mesh=mesh,
        in_specs=(P("dp", "vocab"), P("dp", "vocab"), P(None, "vocab"), P("dp"), P("dp")),
        out_specs=(P("dp"), P("dp", "vocab")),
        check_vma=False,
    )
```

time: 336 us -> 93.8 us (0.28)
  waiting for transfers between devices: 143 us -> 0 us
  blocking collectives: 140 us -> 0 us
  Pallas kernels: 0 us -> 90 us
  matrix products: 31.1 us -> 0 us
  between operations: 14.5 us -> 0.64 us
  other arithmetic: 7.27 us -> 0 us
    all_gather x5 -> x0, blocking collectives: 131 us -> none  [the longest x1 26.6 us: per_device(): lax.all_gather(teacher_local[None, :], 'vocab', axis=0, tiled=True)]
    pallas_call x0 -> x1, Pallas kernels: none -> 90 us  [per_device(): pl.pallas_call(functools.partial(kernel, n, ndp), out_shape=(jax.ShapeDty...]
    reduce_scatter x1 -> x0, waiting for transfers between devices: 86.1 us -> none  [per_device(): lax.psum_scatter(lax.dot_general(head, slopes, (((1,), (1,)), ((), ())),...]
    all_gather x2 -> x0, waiting for transfers between devices: 55.7 us -> none  [the longest x1 42 us: per_device(): lax.all_gather(teacher_hidden, 'vocab', axis=1, tiled=True)]
    dot_general x3 -> x0, matrix products: 31.1 us -> none  [the longest x1 12.8 us: per_device(): lax.dot_general(head, slopes, (((1,), (1,)), ((), ())), preferred_element...]
    psum x1 -> x0, blocking collectives: 9 us -> none  [per_device(): count = lax.psum(jnp.sum(masked), 'dp')]
    reduce_sum x4 -> x0, other arithmetic: 3.43 us -> none  [the longest x1 2.09 us: per_device(): cross_sum = jnp.sum(teacher_exp * (teacher_log - student_log), axis=1)]
  transfers between devices with their start and end apart: 3 -> 0, of which waited for: 3 -> 0; matrix products, arithmetic and copies ran while one was open for 4% -> 0% of each run, Pallas kernels for 0% -> 0%
where the time goes in v1:
time: 93.8 us; the launch traced here: 93.6 us
  Pallas kernels  90 us (96%)
  local copies, waits for them, and re-layouts  2.92 us (3%)
    pallas_call x1, Pallas kernels, per_device(): pl.pallas_call(functools.partial(kernel, n, ndp), out_shape=(jax.ShapeDty...  90 us
    unnamed x2, local copies, waits for them, and re-layouts  2.92 us

profile of v1, /device:TPU:0, one launch (start us, length us, event | category | flops | bytes accessed | tf_op | source)
XLA Modules:
  0.0 93.6 jit_solution(18244361218154174811)
XLA Ops:
  0.6 90.0 %shard_map.68 = (f32[1,512]{1,0:T(1,128)}, bf16[512,256]{1,0:T(8,128)(2,1)}) custom-call(bf16[512,256]{1,0:T(8,128)(2,1)} %s_ref.1, bf16[512,256]{1,0:T(8,128)(2,1)} %t_ref.1, bf16[2048,2048]{1,0:T(8,128)(2,1)} %head_hbm.1, s32[1,512]{1,0:T(1,128)} %bitcast.2, s32[4]{0:T(128)} %steps_ref.1), custom_call_target="tpu_custom_call" | custom-call | tf_op jit(solution)/shard_map/pallas_call | solution.py:295
  90.7 1.2 %copy.9 = f32[512]{0:T(512)} copy(f32[512]{0:T(512)} %bitcast.3) | data formatting | bytes 4096
  91.9 1.7 %copy.10 = bf16[512,256]{1,0:T(8,128)(2,1)} copy(bf16[512,256]{1,0:T(8,128)(2,1)} %get-tuple-element.9) | data formatting | bytes 524288

commit v2 on v1

v2 whole, which is shorter than its diff:
```python
import functools

import jax
import jax.numpy as jnp
from jax import lax
from jax.experimental import pallas as pl
from jax.experimental.pallas import tpu as pltpu
from jax.sharding import PartitionSpec as P

MESH = pl.DeviceIdType.MESH
STEPS = 8
F32, BF16 = jnp.float32, jnp.bfloat16


def loop(start, stop, body):
    lax.fori_loop(start, stop, lambda i, carry: (body(i), carry)[1], 0)


def kernel(
    n, ndp, s_ref, t_ref, head_hbm, mask_ref, steps_ref, div_ref, grad_ref,
    head, s_all, t_all, s_log, t_log, slopes, cols, stats, counts, g, rs_out, rs_in,
    head_sem, ag_send, ag_recv, st_send, st_recv, ct_send, ct_recv, rs_send, rs_recv,
):
    T, F = s_ref.shape
    V = head.shape[1]
    H = n // 2
    C = T // 2
    E = C // 2
    me = lax.axis_index("vocab")
    dp = lax.axis_index("dp")

    def at_pos(q):
        q = lax.rem(q + 2 * n, n)
        x = q // H
        z = q + x * (n - 1 - 2 * q)
        return 2 * z + x

    z0, x0 = me // 2, lax.rem(me, 2)
    pos = z0 + x0 * (n - 1 - 2 * z0)
    ways = ((1, at_pos(pos + 1)), (-1, at_pos(pos - 1)))

    head_copy = pltpu.make_async_copy(head_hbm, head, head_sem)
    head_copy.start()

    count = jnp.sum(mask_ref[...].astype(F32), axis=1, keepdims=True)
    counts[dp] = jnp.broadcast_to(count, counts.shape[1:])

    barrier = pltpu.get_barrier_semaphore()
    for j in range(1, n):
        pl.semaphore_signal(barrier, 1, device_id={"vocab": lax.rem(me + j, n)}, device_id_type=MESH)
    for j in range(1, ndp):
        pl.semaphore_signal(barrier, 1, device_id={"dp": lax.rem(dp + j, ndp)}, device_id_type=MESH)
    pl.semaphore_wait(barrier, n - 1 + ndp - 1)

    def hop(a, way, h, which):
        step, target = ways[way]
        block = at_pos(pos - step * (h - 1))
        everything, own = ((s_all, s_ref), (t_all, t_ref))[which]
        source = own.at[a * C:(a + 1) * C] if isinstance(h, int) and h == 1 else everything.at[a, block]
        return pltpu.make_async_remote_copy(
            src_ref=source,
            dst_ref=everything.at[a, block],
            send_sem=ag_send.at[a, way, h, which],
            recv_sem=ag_recv.at[a, way, h, which],
            device_id={"vocab": target},
            device_id_type=MESH,
        )

    def arrived(a, way, h, which):
        hop(a, way, h, which).wait_recv()
        return at_pos(pos - ways[way][0] * h)

    def begin(a):
        for which in (0, 1):
            for way in (0, 1):
                hop(a, way, 1, which).start()

    begin(0)

    def count_copy(j):
        return pltpu.make_async_remote_copy(
            src_ref=counts.at[dp],
            dst_ref=counts.at[dp],
            send_sem=ct_send.at[j],
            recv_sem=ct_recv.at[j],
            device_id={"dp": lax.rem(dp + j, ndp)},
            device_id_type=MESH,
        )

    for j in range(1, ndp):
        count_copy(j).start()

    W = 256
    logs = (s_log, t_log)
    alls = (s_all, t_all)

    def rows_of(block):
        return pl.ds(pl.multiple_of(block * F, F), F)

    def accumulate(a, log, blocks, everything):
        half = slice(a * C, (a + 1) * C)

        def tile(c):
            span = pl.ds(pl.multiple_of(c * W, W), W)
            total = log[half, span]
            for block in blocks:
                total = total + jnp.dot(
                    everything[a, block], head[rows_of(block), span], preferred_element_type=F32
                )
            log[half, span] = total

        loop(0, V // W, tile)

    def first(log, own):
        def tile(c):
            span = pl.ds(pl.multiple_of(c * W, W), W)
            log[:, span] = jnp.dot(own[...], head[rows_of(me), span], preferred_element_type=F32)

        loop(0, V // W, tile)

    def take(a, h, which):
        found = []
        for way in (0, 1):
            if isinstance(h, int) and h == H and way != which:
                continue
            found.append(arrived(a, way, h, which))
            if isinstance(h, int):
                if h < H and (way == which or h + 1 < H):
                    hop(a, way, h + 1, which).start()
            else:
                hop(a, way, h + 1, which).start()
        accumulate(a, logs[which], found, alls[which])

    R = 16
    lane = lax.broadcasted_iota(jnp.int32, (R, 128), 1)

    def softmax_rows(r):
        span = pl.ds(pl.multiple_of(r * R, R), R)
        s, t = s_log[span, :], t_log[span, :]
        s_peak = jnp.max(s, axis=1, keepdims=True)
        t_peak = jnp.max(t, axis=1, keepdims=True)
        s_exp = jnp.exp(s - s_peak)
        t_exp = jnp.exp(t - t_peak)
        cross = jnp.sum(t_exp * (t - s), axis=1, keepdims=True)
        s_log[span, :] = s_exp
        t_log[span, :] = t_exp
        s_sum = jnp.sum(s_exp, axis=1, keepdims=True)
        t_sum = jnp.sum(t_exp, axis=1, keepdims=True)
        value = jnp.where(lane == 0, s_peak, jnp.where(lane == 1, s_sum, jnp.where(
            lane == 2, t_peak, jnp.where(lane == 3, t_sum, cross))))
        cols[span, :] = value

    def softmax(a, part):
        loop((a * C + part * E) // R, (a * C + part * E + E) // R, softmax_rows)

    def stat_copy(a, j):
        return pltpu.make_async_remote_copy(
            src_ref=stats.at[a, me],
            dst_ref=stats.at[a, me],
            send_sem=st_send.at[a, j],
            recv_sem=st_recv.at[a, j],
            device_id={"vocab": lax.rem(me + j, n)},
            device_id_type=MESH,
        )

    def tell(a):
        stats[a, me] = cols[a * C:(a + 1) * C, :].T[:8, :]
        for j in range(1, n):
            stat_copy(a, j).start()

    def slope_rows(r):
        span = pl.ds(pl.multiple_of(r * R, R), R)
        slopes[span, :] = (s_log[span, :] * cols[span, 0:1] - t_log[span, :] * cols[span, 1:2]).astype(BF16)

    def merge(a):
        half = slice(a * C, (a + 1) * C)
        if a == 0:
            for j in range(1, ndp):
                count_copy(j).wait_recv()
        total = counts[0, :1, :1]
        for j in range(1, ndp):
            total = total + counts[j, :1, :1]
        segments = steps_ref.shape[0] // 2
        factor = jnp.concatenate(
            [
                STEPS / jnp.full((1, C // segments), steps_ref[a * segments + i], jnp.int32).astype(F32)
                for i in range(segments)
            ],
            axis=1,
        )
        weight = mask_ref[:, half].astype(F32) * factor * (T * ndp / jnp.maximum(total, 1.0))
        for j in range(1, n):
            stat_copy(a, j).wait_recv()
        s_top = stats[a, 0, 0:1, :]
        t_top = stats[a, 0, 2:3, :]
        for k in range(1, n):
            s_top = jnp.maximum(s_top, stats[a, k, 0:1, :])
            t_top = jnp.maximum(t_top, stats[a, k, 2:3, :])
        s_total = jnp.zeros((1, C), F32)
        t_total = jnp.zeros((1, C), F32)
        cross = jnp.zeros((1, C), F32)
        for k in range(n):
            t_scale = jnp.exp(stats[a, k, 2:3, :] - t_top)
            s_total += stats[a, k, 1:2, :] * jnp.exp(stats[a, k, 0:1, :] - s_top)
            t_total += stats[a, k, 3:4, :] * t_scale
            cross += stats[a, k, 4:5, :] * t_scale
        div_ref[:, half] = cross / t_total - (t_top + jnp.log(t_total)) + (s_top + jnp.log(s_total))
        mine = stats[a, me]
        s_factor = weight * (jnp.exp(mine[0:1, :] - s_top) / s_total)
        t_factor = weight * (jnp.exp(mine[2:3, :] - t_top) / t_total)
        row = lax.broadcasted_iota(jnp.int32, (128, C), 0)
        cols[half, :] = jnp.where(row == 0, s_factor, t_factor).T
        loop(a * C // R, (a + 1) * C // R, slope_rows)

    def part(a, block):
        return lax.dot_general(
            slopes[a * C:(a + 1) * C, :], head[rows_of(block), :], (((1,), (1,)), ((), ())),
            preferred_element_type=F32,
        )

    def pass_on(a, way, k, c):
        return pltpu.make_async_remote_copy(
            src_ref=rs_out.at[a, way, k, c],
            dst_ref=rs_in.at[a, way, k, c],
            send_sem=rs_send.at[a, way, k, c],
            recv_sem=rs_recv.at[a, way, k, c],
            device_id={"vocab": ways[way][1]},
            device_id_type=MESH,
        )

    def far(a):
        whole = part(a, at_pos(pos + H)).astype(BF16)
        for c in (0, 1):
            rs_out[a, c, H, c] = whole[c * E:(c + 1) * E]
            pass_on(a, c, H, c).start()

    def fill(a, k):
        for way in (0, 1):
            whole = part(a, at_pos(pos + ways[way][0] * k))
            g[way, k, 0] = whole[:E]
            g[way, k, 1] = whole[E:]

    def own(a):
        whole = part(a, me)
        g[0, 0, 0] = whole[:E]
        g[0, 0, 1] = whole[E:]

    def relay_top(a):
        k = H - 1
        for way in (0, 1):
            c = 1 - way
            rs_out[a, way, k, c] = g[way, k, c].astype(BF16)
            pass_on(a, way, k, c).start()
        for way in (0, 1):
            pass_on(a, way, H, way).wait_recv()
            rs_out[a, way, k, way] = (g[way, k, way] + rs_in[a, way, H, way].astype(F32)).astype(BF16)
            pass_on(a, way, k, way).start()

    def relay(a, k):
        for late in (0, 1):
            for way in (0, 1):
                c = 1 - way if late == 0 else way
                pass_on(a, way, k + 1, c).wait_recv()
                rs_out[a, way, k, c] = (g[way, k, c] + rs_in[a, way, k + 1, c].astype(F32)).astype(BF16)
                pass_on(a, way, k, c).start()

    def finish(a):
        for c in (0, 1):
            for way in (0, 1):
                pass_on(a, way, 1, c).wait_recv()
            grad_ref[a * C + c * E:a * C + (c + 1) * E, :] = (
                g[0, 0, c] + rs_in[a, 0, 1, c].astype(F32) + rs_in[a, 1, 1, c].astype(F32)
            ).astype(BF16)

    head_copy.wait()
    first(s_log, s_ref)
    first(t_log, t_ref)

    loop(1, H - 1, lambda h: [take(0, h, which) for which in (0, 1)])
    for which in (0, 1):
        take(0, H - 1, which)
    begin(1)
    for which in (0, 1):
        take(0, H, which)

    take(1, 1, 0)
    softmax(0, 0)
    take(1, 1, 1)
    softmax(0, 1)
    tell(0)
    loop(2, H - 1, lambda h: [take(1, h, which) for which in (0, 1)])
    take(1, H - 1, 0)
    merge(0)
    take(1, H - 1, 1)
    far(0)
    fill(0, H - 1)
    take(1, H, 0)
    loop(1, H - 1, lambda k: fill(0, k))
    take(1, H, 1)
    relay_top(0)

    lower = list(range(H - 2, 0, -1))
    cut = len(lower) // 2
    softmax(1, 0)
    for k in lower[:cut]:
        relay(0, k)
    softmax(1, 1)
    tell(1)
    for k in lower[cut:]:
        relay(0, k)
    own(0)
    merge(1)
    far(1)
    finish(0)
    fill(1, H - 1)
    relay_top(1)

    def rest(i):
        fill(1, H - 2 - i)
        relay(1, H - 2 - i)

    loop(0, H - 2, rest)
    own(1)
    finish(1)

    for a in (0, 1):
        def left(h):
            for way in (0, 1):
                for which in (0, 1):
                    hop(a, way, h, which).wait_send()

        def gone(k):
            for way in (0, 1):
                for c in (0, 1):
                    pass_on(a, way, k, c).wait_send()

        left(1)
        loop(2, H, left)
        loop(1, H, gone)
        for way in (0, 1):
            hop(a, way, H, way).wait_send()
            pass_on(a, way, H, way).wait_send()
        for j in range(1, n):
            stat_copy(a, j).wait_send()
    for j in range(1, ndp):
        count_copy(j).wait_send()


def solution(mesh):
    n, ndp = mesh.shape["vocab"], mesh.shape["dp"]

    def per_device(student, teacher, head, mask, steps):
        T, F = student.shape
        D, V = head.shape
        H = n // 2
        vmem = pl.BlockSpec(memory_space=pltpu.VMEM)
        dma = pltpu.SemaphoreType.DMA
        div, grad = pl.pallas_call(
            functools.partial(kernel, n, ndp),
            out_shape=(jax.ShapeDtypeStruct((1, T), F32), jax.ShapeDtypeStruct((T, F), BF16)),
            in_specs=[vmem, vmem, pl.BlockSpec(memory_space=pl.ANY), vmem, pl.BlockSpec(memory_space=pltpu.SMEM)],
            out_specs=(vmem, vmem),
            scratch_shapes=[
                pltpu.VMEM((D, V), BF16),
                pltpu.VMEM((2, n, T // 2, F), BF16),
                pltpu.VMEM((2, n, T // 2, F), BF16),
                pltpu.VMEM((T, V), F32),
                pltpu.VMEM((T, V), F32),
                pltpu.VMEM((T, V), BF16),
                pltpu.VMEM((T, 128), F32),
                pltpu.VMEM((2, n, 8, T // 2), F32),
                pltpu.VMEM((ndp, 8, 128), F32),
                pltpu.VMEM((2, H, 2, T // 4, F), F32),
                pltpu.VMEM((2, 2, H + 1, 2, T // 4, F), BF16),
                pltpu.VMEM((2, 2, H + 1, 2, T // 4, F), BF16),
                dma,
                dma((2, 2, H + 1, 2)),
                dma((2, 2, H + 1, 2)),
                dma((2, n)),
                dma((2, n)),
                dma((ndp,)),
                dma((ndp,)),
                dma((2, 2, H + 1, 2)),
                dma((2, 2, H + 1, 2)),
            ],
            compiler_params=pltpu.CompilerParams(
                collective_id=0, has_side_effects=True, vmem_limit_bytes=60 * 1024 * 1024
            ),
        )(student, teacher, head, mask.reshape(1, T), steps)
        return div.reshape(T), grad

    return jax.shard_map(
        per_device,
        mesh=mesh,
        in_specs=(P("dp", "vocab"), P("dp", "vocab"), P(None, "vocab"), P("dp"), P("dp")),
        out_specs=(P("dp"), P("dp", "vocab")),
        check_vma=False,
    )
```

time: 93.8 us -> 93.2 us (level)
  no operation moved by 1% of the time
where the time goes in v2:
time: 93.2 us; the launch traced here: 93 us
  Pallas kernels  89.5 us (96%)
  local copies, waits for them, and re-layouts  2.92 us (3%)
    pallas_call x1, Pallas kernels, per_device(): pl.pallas_call(functools.partial(kernel, n, ndp), out_shape=(jax.ShapeDty...  89.5 us
    unnamed x2, local copies, waits for them, and re-layouts  2.92 us

profile of v2, /device:TPU:0, one launch (start us, length us, event | category | flops | bytes accessed | tf_op | source)
XLA Modules:
  0.0 93.0 jit_solution(137207119191648525)
XLA Ops:
  0.6 89.5 %shard_map.68 = (f32[1,512]{1,0:T(1,128)}, bf16[512,256]{1,0:T(8,128)(2,1)}) custom-call(bf16[512,256]{1,0:T(8,128)(2,1)} %s_ref.1, bf16[512,256]{1,0:T(8,128)(2,1)} %t_ref.1, bf16[2048,2048]{1,0:T(8,128)(2,1)} %head_hbm.1, s32[1,512]{1,0:T(1,128)} %bitcast.2, s32[4]{0:T(128)} %steps_ref.1), custom_call_target="tpu_custom_call" | custom-call | tf_op jit(solution)/shard_map/pallas_call | solution.py:358
  90.1 1.2 %copy.9 = f32[512]{0:T(512)} copy(f32[512]{0:T(512)} %bitcast.3) | data formatting | bytes 4096
  91.4 1.7 %copy.10 = bf16[512,256]{1,0:T(8,128)(2,1)} copy(bf16[512,256]{1,0:T(8,128)(2,1)} %get-tuple-element.9) | data formatting | bytes 524288

commit v3 on v2

--- a/solution.py
+++ b/solution.py
@@ -12,8 +12,8 @@
 F32, BF16 = jnp.float32, jnp.bfloat16
 
 
-def loop(start, stop, body):
-    lax.fori_loop(start, stop, lambda i, carry: (body(i), carry)[1], 0)
+def loop(start, stop, body, unroll=1):
+    lax.fori_loop(start, stop, lambda i, carry: (body(i), carry)[1], 0, unroll=unroll)
 
 
 def kernel(
@@ -90,7 +90,7 @@
     for j in range(1, ndp):
         count_copy(j).start()
 
-    W = 256
+    W, U = 256, 4
     logs = (s_log, t_log)
     alls = (s_all, t_all)
 
@@ -100,23 +100,25 @@
     def accumulate(a, log, blocks, everything):
         half = slice(a * C, (a + 1) * C)
 
-        def tile(c):
-            span = pl.ds(pl.multiple_of(c * W, W), W)
-            total = log[half, span]
-            for block in blocks:
-                total = total + jnp.dot(
-                    everything[a, block], head[rows_of(block), span], preferred_element_type=F32
-                )
-            log[half, span] = total
-
-        loop(0, V // W, tile)
+        def tile(i):
+            for u in range(U):
+                span = pl.ds(pl.multiple_of((i * U + u) * W, W), W)
+                total = log[half, span]
+                for block in blocks:
+                    total = total + jnp.dot(
+                        everything[a, block], head[rows_of(block), span], preferred_element_type=F32
+                    )
+                log[half, span] = total
+
+        loop(0, V // (W * U), tile)
 
     def first(log, own):
-        def tile(c):
-            span = pl.ds(pl.multiple_of(c * W, W), W)
-            log[:, span] = jnp.dot(own[...], head[rows_of(me), span], preferred_element_type=F32)
-
-        loop(0, V // W, tile)
+        def tile(i):
+            for u in range(U):
+                span = pl.ds(pl.multiple_of((i * U + u) * W, W), W)
+                log[:, span] = jnp.dot(own[...], head[rows_of(me), span], preferred_element_type=F32)
+
+        loop(0, V // (W * U), tile)
 
     def take(a, h, which):
         found = []
@@ -151,7 +153,7 @@
         cols[span, :] = value
 
     def softmax(a, part):
-        loop((a * C + part * E) // R, (a * C + part * E + E) // R, softmax_rows)
+        loop((a * C + part * E) // R, (a * C + part * E + E) // R, softmax_rows, 2)
 
     def stat_copy(a, j):
         return pltpu.make_async_remote_copy(
@@ -210,7 +212,7 @@
         t_factor = weight * (jnp.exp(mine[2:3, :] - t_top) / t_total)
         row = lax.broadcasted_iota(jnp.int32, (128, C), 0)
         cols[half, :] = jnp.where(row == 0, s_factor, t_factor).T
-        loop(a * C // R, (a + 1) * C // R, slope_rows)
+        loop(a * C // R, (a + 1) * C // R, slope_rows, 4)
 
     def part(a, block):
         return lax.dot_general(

time: 93.2 us -> 87.3 us (0.937)
  Pallas kernels: 89.5 us -> 83.6 us
    pallas_call x1, Pallas kernels: 89.5 us -> 83.6 us  [per_device(): pl.pallas_call(functools.partial(kernel, n, ndp), out_shape=(jax.ShapeDty...]
where the time goes in v3:
time: 87.3 us; the launch traced here: 87.1 us
  Pallas kernels  83.6 us (96%)
  local copies, waits for them, and re-layouts  2.92 us (3%)
    pallas_call x1, Pallas kernels, per_device(): pl.pallas_call(functools.partial(kernel, n, ndp), out_shape=(jax.ShapeDty...  83.6 us
    unnamed x2, local copies, waits for them, and re-layouts  2.92 us

profile of v3, /device:TPU:0, one launch (start us, length us, event | category | flops | bytes accessed | tf_op | source)
XLA Modules:
  0.0 87.1 jit_solution(11861360377341831442)
XLA Ops:
  0.6 83.6 %shard_map.68 = (f32[1,512]{1,0:T(1,128)}, bf16[512,256]{1,0:T(8,128)(2,1)}) custom-call(bf16[512,256]{1,0:T(8,128)(2,1)} %s_ref.1, bf16[512,256]{1,0:T(8,128)(2,1)} %t_ref.1, bf16[2048,2048]{1,0:T(8,128)(2,1)} %head_hbm.1, s32[1,512]{1,0:T(1,128)} %bitcast.2, s32[4]{0:T(128)} %steps_ref.1), custom_call_target="tpu_custom_call" | custom-call | tf_op jit(solution)/shard_map/pallas_call | solution.py:360
  84.2 1.2 %copy.9 = f32[512]{0:T(512)} copy(f32[512]{0:T(512)} %bitcast.3) | data formatting | bytes 4096
  85.5 1.7 %copy.10 = bf16[512,256]{1,0:T(8,128)(2,1)} copy(bf16[512,256]{1,0:T(8,128)(2,1)} %get-tuple-element.9) | data formatting | bytes 524288

commit v4 on v3

--- a/solution.py
+++ b/solution.py
@@ -302,18 +302,16 @@
     relay_top(0)
 
     lower = list(range(H - 2, 0, -1))
-    cut = len(lower) // 2
     softmax(1, 0)
-    for k in lower[:cut]:
-        relay(0, k)
     softmax(1, 1)
     tell(1)
-    for k in lower[cut:]:
+    for k in lower[:-1]:
         relay(0, k)
     own(0)
     merge(1)
     far(1)
-    finish(0)
+    for k in lower[-1:]:
+        relay(0, k)
     fill(1, H - 1)
     relay_top(1)
 
@@ -322,6 +320,7 @@
         relay(1, H - 2 - i)
 
     loop(0, H - 2, rest)
+    finish(0)
     own(1)
     finish(1)
 

time: 87.3 us -> 85.2 us (0.976)
  Pallas kernels: 83.6 us -> 81.5 us
    pallas_call x1, Pallas kernels: 83.6 us -> 81.5 us  [per_device(): pl.pallas_call(functools.partial(kernel, n, ndp), out_shape=(jax.ShapeDty...]
where the time goes in v4:
time: 85.2 us; the launch traced here: 85 us
  Pallas kernels  81.5 us (96%)
  local copies, waits for them, and re-layouts  2.92 us (3%)
    pallas_call x1, Pallas kernels, per_device(): pl.pallas_call(functools.partial(kernel, n, ndp), out_shape=(jax.ShapeDty...  81.5 us
    unnamed x2, local copies, waits for them, and re-layouts  2.92 us

profile of v4, /device:TPU:0, one launch (start us, length us, event | category | flops | bytes accessed | tf_op | source)
XLA Modules:
  0.0 85.0 jit_solution(8107604264025798039)
XLA Ops:
  0.6 81.5 %shard_map.68 = (f32[1,512]{1,0:T(1,128)}, bf16[512,256]{1,0:T(8,128)(2,1)}) custom-call(bf16[512,256]{1,0:T(8,128)(2,1)} %s_ref.1, bf16[512,256]{1,0:T(8,128)(2,1)} %t_ref.1, bf16[2048,2048]{1,0:T(8,128)(2,1)} %head_hbm.1, s32[1,512]{1,0:T(1,128)} %bitcast.2, s32[4]{0:T(128)} %steps_ref.1), custom_call_target="tpu_custom_call" | custom-call | tf_op jit(solution)/shard_map/pallas_call | solution.py:359
  82.1 1.2 %copy.9 = f32[512]{0:T(512)} copy(f32[512]{0:T(512)} %bitcast.3) | data formatting | bytes 4096
  83.3 1.7 %copy.10 = bf16[512,256]{1,0:T(8,128)(2,1)} copy(bf16[512,256]{1,0:T(8,128)(2,1)} %get-tuple-element.9) | data formatting | bytes 524288
